TPU v7x, 256 devices: a whole 4x4x8 slice. The times are simulated.
256 devices in a mesh: src: 8 (over y, core), snk: 32 (over x, z).
Axes of the slice: x: 4, y: 4, z: 8, core: 2. Of those that a mesh axis runs over, the one named last changes fastest.
Arguments:
- peram: bfloat16 [8, 32, 2, 256, 256], P('src', None, None, None, 'snk'), may hold values from -6 to 6
- meson_blocks: bfloat16 [32, 4, 2, 256, 256], P('snk'), may hold values from -0.25 to 0.25
- edge_left: int32 [8, 32, 32], P('src', 'snk'), may hold values from 0 to 3
- edge_right: int32 [8, 32, 32], P('src', 'snk'), may hold values from 0 to 3
- edge_node: int32 [8, 32, 32], P('src', 'snk'), may hold values from 0 to 4
- edge_weight: int32 [8, 32, 32], P('src', 'snk'), may hold values from 0 to 15
- weight_table: float32 [16, 2], replicated, may hold values from -0.2 to 0.2
Outputs:
- node_matrices: bfloat16 [256, 4, 2, 256], P('snk')
Inputs may be any that keep to these rules, and one draw needn't show every extreme that they name: `edge_node`: the value 4 marks an empty slot that feeds no node.
All inputs are finite; a program needn't handle non-finite values.
Results may differ from a plain program's by a relative error of at most 0.009.
Values may be sent and summed in bfloat16 or wider, within the bound.
No kernel may reach another device: no remote copies, remote signals or barrier semaphores. Data moves between devices by JAX's collectives and lax.ppermute only.
A program may use at most 128 MiB of HBM per device.

v0:
```python
import functools

import jax
import jax.numpy as jnp
from jax import lax
from jax.experimental import pallas as pl
from jax.experimental.pallas import tpu as pltpu
from jax.sharding import Mesh, PartitionSpec as P


N = 256
MOM = 4
EDGES = 32
NODES = 4
SNK = 32
ROWS = N // SNK
DEEP = MOM * 2 * N
ALL = ("y", "core", "x", "z")
NY, NC, NX, NZ = 4, 2, 4, 8
BF16 = jnp.bfloat16
F32 = jnp.float32
VMEM_CAP = 14 * 2**20
CHUNK = 64
POSTS = (0, 3)
LINES = ((1, 4), (7, 2), (6, 5))
MIX_CAP = (8 * 2**20, 60 * 2**20)
ROUND = (1, 3, 2)


def mix_kernel(keep, left_e, right_e, node_e, weight_e, table, blocks, out, gain):
    core = lax.axis_index("core")
    first = 2 * (core if keep else 1 - core)
    shift = lax.axis_index("x") - lax.axis_index("y") + 2 * NX

    @pl.when(pl.program_id(0) == 0)
    def fold_edges():
        def clear(i, carry):
            gain[0, i] = 0.0
            gain[1, i] = 0.0
            return carry

        lax.fori_loop(0, (NODES + 1) * 16, clear, 0)

        def gather(e, carry):
            key = node_e[0, 0, e] * 16 + right_e[0, 0, e] * 4 + left_e[0, 0, e]
            w = weight_e[0, 0, e]
            gain[0, key] = gain[0, key] + table[0, w]
            gain[1, key] = gain[1, key] + table[1, w]
            return carry

        lax.fori_loop(0, EDGES, gather, 0)

    step = 16

    def rows(r, carry):
        here = pl.ds(pl.multiple_of(r * step, step), step)
        real = [blocks[0, a, 0, here, :].astype(F32) for a in range(MOM)]
        imag = [blocks[0, a, 1, here, :].astype(F32) for a in range(MOM)]
        both = [u + v for u, v in zip(real, imag)]
        for n in range(2):
            for d in range(MOM):
                base = (first + n) * 16 + lax.rem(shift - d, MOM) * 4
                wr = [gain[0, base + a] for a in range(MOM)]
                wi = [gain[1, base + a] for a in range(MOM)]
                mid = sum(wr[a] * both[a] for a in range(1, MOM)) + wr[0] * both[0]
                low = sum((wr[a] + wi[a]) * imag[a] for a in range(1, MOM))
                low = low + (wr[0] + wi[0]) * imag[0]
                top = sum((wi[a] - wr[a]) * real[a] for a in range(1, MOM))
                top = top + (wi[0] - wr[0]) * real[0]
                out[n, here, (2 * d) * N : (2 * d + 1) * N] = (mid - low).astype(BF16)
                out[n, here, (2 * d + 1) * N : (2 * d + 2) * N] = (mid + top).astype(BF16)
        return carry

    lax.fori_loop(0, CHUNK // step, rows, 0)


def mix(keep, left, right, node, weight, table, blocks):
    smem = pl.BlockSpec(memory_space=pltpu.SMEM)
    half = pl.BlockSpec((2, CHUNK, DEEP), lambda i: (0, i, 0))
    return pl.pallas_call(
        functools.partial(mix_kernel, keep),
        grid=(N // CHUNK,),
        out_shape=jax.ShapeDtypeStruct((NODES if keep else 2, N, DEEP), BF16),
        in_specs=[smem] * 5 + [pl.BlockSpec((1, MOM, 2, CHUNK, N), lambda i: (0, 0, 0, i, 0))],
        out_specs=half,
        scratch_shapes=[pltpu.SMEM((2, 128), F32)],
        compiler_params=pltpu.CompilerParams(vmem_limit_bytes=MIX_CAP[keep]),
        cost_estimate=pl.CostEstimate(
            flops=2 * MOM * MOM * 8 * N * N,
            bytes_accessed=(MOM * 2 + 2 * MOM * 2) * N * N * 2,
            transcendentals=0,
        ),
        name="mix_keep" if keep else "mix_send",
    )(left, right, node, weight, table, blocks)


def half_product(mixed, stack, out):
    parts = [
        jnp.dot(mixed[n], stack[...], preferred_element_type=F32).reshape(SNK, ROWS, 2 * N)
        for n in range(2)
    ]
    out[...] = jnp.concatenate(parts, 1).astype(out.dtype)


def send_kernel(tau_t, r0, r1, r2, r3, mixed, send, stack):
    tau = [
        tau_t[:, p].astype(F32).reshape(N, N).T.astype(BF16) for p in range(2)
    ]
    for d, block in enumerate((r0, r1, r2, r3)):
        real = jnp.dot(tau[0], block[0], preferred_element_type=F32) - jnp.dot(
            tau[1], block[1], preferred_element_type=F32
        )
        imag = jnp.dot(tau[0], block[1], preferred_element_type=F32) + jnp.dot(
            tau[1], block[0], preferred_element_type=F32
        )
        top, low = 2 * d * N, (2 * d + 1) * N
        stack[top : top + N, :N] = real.astype(BF16)
        stack[top : top + N, N:] = imag.astype(BF16)
        stack[low : low + N, :N] = (-imag).astype(BF16)
        stack[low : low + N, N:] = real.astype(BF16)
    half_product(mixed, stack, send)


def send_half(tau_t, right, mixed):
    vmem = pl.BlockSpec(memory_space=pltpu.VMEM)
    return pl.pallas_call(
        send_kernel,
        out_shape=(
            jax.ShapeDtypeStruct((SNK, 2 * ROWS, 2 * N), BF16),
            jax.ShapeDtypeStruct((DEEP, 2 * N), BF16),
        ),
        in_specs=[vmem] * 6,
        out_specs=(vmem, vmem),
        compiler_params=pltpu.CompilerParams(vmem_limit_bytes=VMEM_CAP),
        cost_estimate=pl.CostEstimate(
            flops=2 * (MOM * 4 + 2 * MOM * 4) * N * N * N,
            bytes_accessed=6 * 2**20,
            transcendentals=0,
        ),
        name="send_half",
    )(tau_t, *right, mixed)


def keep_half(mixed, stack):
    vmem = pl.BlockSpec(memory_space=pltpu.VMEM)
    return pl.pallas_call(
        half_product,
        out_shape=jax.ShapeDtypeStruct((SNK, 2 * ROWS, 2 * N), F32),
        in_specs=[vmem] * 2,
        out_specs=vmem,
        compiler_params=pltpu.CompilerParams(vmem_limit_bytes=VMEM_CAP),
        cost_estimate=pl.CostEstimate(
            flops=2 * 2 * MOM * 4 * N * N * N,
            bytes_accessed=5 * 2**20,
            transcendentals=0,
        ),
        name="keep_half",
    )(mixed, stack)


def device(y, c, x, z):
    return ((y * NC + c) * NX + x % NX) * NZ + z % NZ


def spread(block):
    y = lax.axis_index("y")
    lines = [(a, c, b) for a in range(NY) for c in range(NC) for b in range(NX)]
    own = lax.dynamic_index_in_dim(block, y, 0, keepdims=False)
    turns = [
        (device(b, (c + e) % NC, a, 4 * c), device(a, c, a + b, 4 * c + d))
        for a, c, b in lines
        for e, d in enumerate(POSTS)
    ]
    got = [lax.ppermute(own, ALL, turns)]
    for hops in LINES:
        pairs = [
            (device(a, c, b, 4 * c + post), device(a, c, b, 4 * c + d))
            for a, c, b in lines
            for post, d in zip(POSTS, hops)
        ]
        got.append(lax.ppermute(got[0], ALL, pairs))
    part = functools.reduce(jnp.add, got)
    pieces = {0: part}
    for d in ROUND:
        pieces[d] = lax.ppermute(part, "x", [(i, (i + d) % NX) for i in range(NX)])
    return [pieces[d] for d in range(NX)]


def shards(peram, meson_blocks, edge_left, edge_right, edge_node, edge_weight, weight_table):
    return contract(
        peram,
        meson_blocks,
        (edge_left, edge_right, edge_node, edge_weight, weight_table.T),
    )


def contract(peram, meson_blocks, edges):
    core = lax.axis_index("core")
    by_time = jnp.swapaxes(peram[0], 2, 3)
    tau_t = lax.all_to_all(by_time, ("x", "z"), split_axis=0, concat_axis=0, tiled=True)
    mixed_keep = mix(True, *edges, meson_blocks)
    mixed_send = mix(False, *edges, meson_blocks)
    right = spread(meson_blocks[0])
    send, stack = send_half(tau_t, right, mixed_send)
    got = lax.ppermute(send, "core", [(0, 1), (1, 0)])
    keep = keep_half(mixed_keep, stack)
    pair = (keep + got.astype(F32)).astype(BF16)
    times = lax.all_to_all(pair, ("x", "z"), split_axis=0, concat_axis=0, tiled=True)
    one = jnp.sum(times.astype(F32), 0)
    total = one
    for d in range(1, NY):
        total = total + lax.ppermute(one, "y", [(i, (i + d) % NY) for i in range(NY)])
    mine = total.astype(BF16)
    other = lax.ppermute(mine, "core", [(0, 1), (1, 0)])
    halves = jnp.where(core == 0, jnp.stack([mine, other]), jnp.stack([other, mine]))
    halves = halves.reshape(2, 2, ROWS, 2, N)
    return jnp.transpose(halves, (2, 0, 1, 3, 4)).reshape(ROWS, NODES, 2, N)


def solution(mesh):
    fine = Mesh(mesh.devices.reshape(NY, NC, NX, NZ), ALL)
    src, snk = ("y", "core"), ("x", "z")
    edges = P(src, snk, None)
    return jax.shard_map(
        shards,
        mesh=fine,
        in_specs=(
            P(src, None, None, None, snk),
            P(snk, None, None, None, None),
            edges,
            edges,
            edges,
            edges,
            P(),
        ),
        out_specs=P(snk, None, None, None),
        check_vma=False,
    )
```

profile of v0, /device:TPU:1, one launch (start us, length us, event | category | flops | bytes accessed | tf_op | source)
XLA Modules:
  0.0 95.5 jit_solution(7528600958164955743)
XLA Ops:
  0.0 0.0 copy-start.1
  0.0 0.0 copy-start.8
  0.0 0.0 copy-start.7
  0.0 0.0 copy-start.6
  0.0 0.0 copy-start.5
  0.0 0.0 copy-start.4
  0.1 1.1 %dynamic-slice_bitcast_fusion = bf16[2,256,256]{2,1,0:T(8,128)(2,1)S(1)} fusion(bf16[1,4,2,256,256]{4,3,2,1,0:T(8,128)(2,1)} %blocks.3, s32[]{:T(128)S(6)} %select_n.14), kind=kLoop, calls=%fused_computation.3 | loop fusion | bytes 524292 | tf_op jit(solution)/shard_map/jit(dynamic_index_in_dim)/squeeze | solution.py:168
  1.1 7.6 %collective-permute-start = (bf16[2,256,256]{2,1,0:T(8,128)(2,1)S(1)}, bf16[2,256,256]{2,1,0:T(8,128)(2,1)S(1)}, u32[]{:S(2)}, u32[]{:S(2)}) collective-permute-start(bf16[2,256,256]{2,1,0:T(8,128)(2,1)S(1)} %dynamic-slice_bitcast_fusion), channel_id=1, source_target_pairs={{0,0},{32,3},{64,8},{96,11},{128,16},{160,19},{192,24},{224,27},{3... | collective-permute-start | bytes 786440 | tf_op jit(solution)/shard_map/ppermute | solution.py:174
  8.8 3.3 %collective-permute-done = bf16[2,256,256]{2,1,0:T(8,128)(2,1)S(1)} collective-permute-done((bf16[2,256,256]{2,1,0:T(8,128)(2,1)S(1)}, bf16[2,256,256]{2,1,0:T(8,128)(2,1)S(1)}, u32[]{:S(2)}, u32[]{:S(2)}) %collective-permute-start) | collective-permute-done | bytes 262176 | tf_op jit(solution)/shard_map/ppermute | solution.py:174
  12.0 0.7 collective-permute-start.3
  12.7 0.7 collective-permute-start.2
  13.4 1.3 %collective-permute-start.1 = (bf16[2,256,256]{2,1,0:T(8,128)(2,1)S(1)}, bf16[2,256,256]{2,1,0:T(8,128)(2,1)S(1)}, u32[]{:S(2)}, u32[]{:S(2)}) collective-permute-start(bf16[2,256,256]{2,1,0:T(8,128)(2,1)S(1)} %collective-permute-done), channel_id=1, source_target_pairs={{0,1},{3,4},{8,9},{11,12},{16,17},{19,20},{24,25},{27,28},{36,37},... | collective-permute-start | bytes 786440 | tf_op jit(solution)/shard_map/ppermute | solution.py:181
  14.7 15.2 %all-to-all-start = ((bf16[32,2,8,256]{3,2,1,0:T(8,128)(2,1)}), bf16[32,2,8,256]{3,2,1,0:T(8,128)(2,1)S(1)}, u32[]{:S(2)}, u32[]{:S(2)}) async-start(bf16[32,2,8,256]{3,2,1,0:T(8,128)(2,1)} %bitcast.11), calls=%async_computation | async-start | bytes 524288 | tf_op jit(solution)/shard_map/all_to_all | solution.py:200
  29.9 0.0 collective-permute-done.3
  29.9 0.0 collective-permute-done.2
  29.9 0.0 collective-permute-done.1
  29.9 0.1 add_add_fusion.r0
  30.0 2.6 %collective-permute-start.6 = (bf16[2,256,256]{2,1,0:T(8,128)(2,1)S(1)}, bf16[2,256,256]{2,1,0:T(8,128)(2,1)S(1)}, u32[]{:S(2)}, u32[]{:S(2)}) collective-permute-start(bf16[2,256,256]{2,1,0:T(8,128)(2,1)S(1)} %add_add_fusion.r0), channel_id=1, source_target_pairs={{0,24},{8,0},{16,8},{24,16},{1,25},{9,1},{17,9},{25,17},{2,26},{10... | collective-permute-start | bytes 786440 | tf_op jit(solution)/shard_map/ppermute | solution.py:185
  32.5 0.5 collective-permute-start.5
  33.1 0.6 collective-permute-start.4
  33.7 0.0 copy-done.1
  33.7 0.0 copy-done.8
  33.7 0.0 copy-done.7
  33.7 0.0 copy-done.6
  33.7 0.0 copy-done.5
  33.7 0.0 copy-done.4
  33.7 4.2 %mix_send.1.mixed = bf16[2,256,2048]{2,1,0:T(8,128)(2,1)S(1)} custom-call(s32[1,1,32]{2,1,0:T(1,128)S(1)} %copy-done.5, s32[1,1,32]{2,1,0:T(1,128)S(1)} %copy-done.6, s32[1,1,32]{2,1,0:T(1,128)S(1)} %copy-done.7, s32[1,1,32]{2,1,0:T(1,128)S(1)} %copy-done.8, f32[2,16]{1,0:T(2,128)S(1)} %bitcast.10, bf16[1,4,2,256,256]{4,3,2,1,0:T(8,128)(2,1)S(1)} %copy-done.1), custom_call_target="tpu_custom_call" | custom-call | flops 16777216 | bytes 3145728 | tf_op jit(solution)/shard_map/mix_send/pallas_call | solution.py:80
  37.9 0.0 copy-start.2
  37.9 1.3 %copy-done.2 = bf16[2,256,2048]{2,1,0:T(8,128)(2,1)} copy-done((bf16[2,256,2048]{2,1,0:T(8,128)(2,1)}, bf16[2,256,2048]{2,1,0:T(8,128)(2,1)S(1)}, u32[]{:S(2)}) %copy-start.2) | copy-done | bytes 2097176
  39.2 2.1 %all-to-all-done.tau_t = bf16[32,2,8,256]{3,2,1,0:T(8,128)(2,1)S(1)} async-done(((bf16[32,2,8,256]{3,2,1,0:T(8,128)(2,1)}), bf16[32,2,8,256]{3,2,1,0:T(8,128)(2,1)S(1)}, u32[]{:S(2)}, u32[]{:S(2)}) %all-to-all-start) | async-done | bytes 262176 | tf_op jit(solution)/shard_map/all_to_all | solution.py:200
  41.3 4.9 %collective-permute-done.6.r3 = bf16[2,256,256]{2,1,0:T(8,128)(2,1)S(1)} collective-permute-done((bf16[2,256,256]{2,1,0:T(8,128)(2,1)S(1)}, bf16[2,256,256]{2,1,0:T(8,128)(2,1)S(1)}, u32[]{:S(2)}, u32[]{:S(2)}) %collective-permute-start.6) | collective-permute-done | bytes 262176 | tf_op jit(solution)/shard_map/ppermute | solution.py:185
  46.2 0.0 collective-permute-done.5.r2
  46.2 3.5 %collective-permute-done.4.r1 = bf16[2,256,256]{2,1,0:T(8,128)(2,1)S(1)} collective-permute-done((bf16[2,256,256]{2,1,0:T(8,128)(2,1)S(1)}, bf16[2,256,256]{2,1,0:T(8,128)(2,1)S(1)}, u32[]{:S(2)}, u32[]{:S(2)}) %collective-permute-start.4) | collective-permute-done | bytes 262176 | tf_op jit(solution)/shard_map/ppermute | solution.py:185
  49.7 0.0 copy-start.3
  49.7 1.6 %copy-done.3 = bf16[2,256,2048]{2,1,0:T(8,128)(2,1)S(1)} copy-done((bf16[2,256,2048]{2,1,0:T(8,128)(2,1)S(1)}, bf16[2,256,2048]{2,1,0:T(8,128)(2,1)}, u32[]{:S(2)}) %copy-start.3) | copy-done | bytes 2097176
  51.3 1.8 %send_half.1 = (bf16[32,16,512]{2,1,0:T(8,128)(2,1)S(1)}, bf16[2048,512]{1,0:T(8,128)(2,1)S(1)}) custom-call(bf16[32,2,8,256]{3,2,1,0:T(8,128)(2,1)S(1)} %all-to-all-done.tau_t, bf16[2,256,256]{2,1,0:T(8,128)(2,1)S(1)} %add_add_fusion.r0, bf16[2,256,256]{2,1,0:T(8,128)(2,1)S(1)} %collective-permute-done.4.r1, ...), custom_call_target="tpu_custom_call" | custom-call | flops 1610612736 | bytes 6291456 | tf_op jit(solution)/shard_map/send_half/pallas_call | solution.py:126
  53.2 0.6 collective-permute-start.7
  53.8 5.7 %mix_keep.1.mixed = bf16[4,256,2048]{2,1,0:T(8,128)(2,1)} custom-call(s32[1,1,32]{2,1,0:T(1,128)} %left_e.3, s32[1,1,32]{2,1,0:T(1,128)} %right_e.3, s32[1,1,32]{2,1,0:T(1,128)} %node_e.3, s32[1,1,32]{2,1,0:T(1,128)} %weight_e.3, f32[2,16]{1,0:T(2,128)} %bitcast.9, bf16[1,4,2,256,256]{4,3,2,1,0:T(8,128)(2,1)} %blocks.3), custom_call_target="tpu_custom_call" | custom-call | flops 16777216 | bytes 3145728 | tf_op jit(solution)/shard_map/mix_keep/pallas_call | solution.py:80
  59.4 0.0 copy-start
  59.4 2.2 %copy-done = bf16[4,256,2048]{2,1,0:T(8,128)(2,1)S(1)} copy-done((bf16[4,256,2048]{2,1,0:T(8,128)(2,1)S(1)}, bf16[4,256,2048]{2,1,0:T(8,128)(2,1)}, u32[]{:S(2)}) %copy-start) | copy-done | bytes 4194328
  61.6 1.2 %keep_half.1 = f32[32,16,512]{2,1,0:T(8,128)S(1)} custom-call(bf16[4,256,2048]{2,1,0:T(8,128)(2,1)S(1)} %copy-done, bf16[2048,512]{1,0:T(8,128)(2,1)S(1)} %get-tuple-element.7.stack), custom_call_target="tpu_custom_call" | custom-call | flops 1073741824 | bytes 5242880 | tf_op jit(solution)/shard_map/keep_half/pallas_call | solution.py:146
  62.9 0.0 collective-permute-done.7
  62.9 0.2 add_convert_fusion
  63.1 20.8 %all_to_all.10 = bf16[32,16,512]{2,1,0:T(8,128)(2,1)S(1)} all-to-all(bf16[32,16,512]{2,1,0:T(8,128)(2,1)S(1)} %add_convert_fusion), channel_id=1, replica_groups=mesh['y'=4,'core'=2,'x'=4,'z'=8] {'x','z'}, dimensions={0} | all-to-all | bytes 1048576 | tf_op jit(solution)/shard_map/all_to_all | solution.py:208
  83.9 0.1 convert_reduce_fusion
  84.0 0.1 collective-permute-start.10
  84.1 1.3 %collective-permute-start.9 = (f32[16,512]{1,0:T(8,128)S(1)}, f32[16,512]{1,0:T(8,128)S(1)}, u32[]{:S(2)}, u32[]{:S(2)}) collective-permute-start(f32[16,512]{1,0:T(8,128)S(1)} %convert_reduce_fusion), channel_id=1, source_target_pairs={{0,128},{64,192},{128,0},{192,64},{1,129},{65,193},{129,1},{193,65... | collective-permute-start | bytes 98312 | tf_op jit(solution)/shard_map/ppermute | solution.py:212
  85.4 0.2 collective-permute-start.8
  85.5 1.3 %collective-permute-done.10 = f32[16,512]{1,0:T(8,128)S(1)} collective-permute-done((f32[16,512]{1,0:T(8,128)S(1)}, f32[16,512]{1,0:T(8,128)S(1)}, u32[]{:S(2)}, u32[]{:S(2)}) %collective-permute-start.10) | collective-permute-done | bytes 32800 | tf_op jit(solution)/shard_map/ppermute | solution.py:212
  86.8 1.6 %collective-permute-done.9 = f32[16,512]{1,0:T(8,128)S(1)} collective-permute-done((f32[16,512]{1,0:T(8,128)S(1)}, f32[16,512]{1,0:T(8,128)S(1)}, u32[]{:S(2)}, u32[]{:S(2)}) %collective-permute-start.9) | collective-permute-done | bytes 32800 | tf_op jit(solution)/shard_map/ppermute | solution.py:212
  88.4 0.9 collective-permute-done.8
  89.4 4.6 %collective-permute-start.11 = (bf16[16,512]{1,0:T(8,128)(2,1)S(1)}, bf16[16,512]{1,0:T(8,128)(2,1)S(1)}, u32[]{:S(2)}, u32[]{:S(2)}) collective-permute-start(bf16[16,512]{1,0:T(8,128)(2,1)S(1)} %add_convert_fusion.1), channel_id=1, source_target_pairs={{0,32},{32,0},{1,33},{33,1},{2,34},{34,2},{3,35},{35,3},{4,36},{36... | collective-permute-start | bytes 49160 | tf_op jit(solution)/shard_map/ppermute | solution.py:214
  93.9 0.8 collective-permute-done.11
  94.8 0.1 broadcast_select_fusion
  94.8 0.6 copy.8
  (3 shorter events, 0.0 us)
Async XLA Ops:
  0.0 33.7 %copy-start.1 = (bf16[1,4,2,256,256]{4,3,2,1,0:T(8,128)(2,1)S(1)}, bf16[1,4,2,256,256]{4,3,2,1,0:T(8,128)(2,1)}, u32[]{:S(2)}) copy-start(bf16[1,4,2,256,256]{4,3,2,1,0:T(8,128)(2,1)} %blocks.3) | copy-start | bytes 3145732
  0.0 33.7 %copy-start.8 = (s32[1,1,32]{2,1,0:T(1,128)S(1)}, s32[1,1,32]{2,1,0:T(1,128)}, u32[]{:S(2)}) copy-start(s32[1,1,32]{2,1,0:T(1,128)} %weight_e.3) | copy-start | bytes 388
  0.0 33.7 %copy-start.7 = (s32[1,1,32]{2,1,0:T(1,128)S(1)}, s32[1,1,32]{2,1,0:T(1,128)}, u32[]{:S(2)}) copy-start(s32[1,1,32]{2,1,0:T(1,128)} %node_e.3) | copy-start | bytes 388
  0.0 33.7 %copy-start.6 = (s32[1,1,32]{2,1,0:T(1,128)S(1)}, s32[1,1,32]{2,1,0:T(1,128)}, u32[]{:S(2)}) copy-start(s32[1,1,32]{2,1,0:T(1,128)} %right_e.3) | copy-start | bytes 388
  0.0 33.6 %copy-start.5 = (s32[1,1,32]{2,1,0:T(1,128)S(1)}, s32[1,1,32]{2,1,0:T(1,128)}, u32[]{:S(2)}) copy-start(s32[1,1,32]{2,1,0:T(1,128)} %left_e.3) | copy-start | bytes 388
  0.0 33.6 %copy-start.4 = (f32[16,2]{0,1:T(2,128)S(1)}, f32[16,2]{0,1:T(2,128)}, u32[]{:S(2)}) copy-start(f32[16,2]{0,1:T(2,128)} %param.13) | copy-start | bytes 388
  1.1 10.9 %collective-permute-start = (bf16[2,256,256]{2,1,0:T(8,128)(2,1)S(1)}, bf16[2,256,256]{2,1,0:T(8,128)(2,1)S(1)}, u32[]{:S(2)}, u32[]{:S(2)}) collective-permute-start(bf16[2,256,256]{2,1,0:T(8,128)(2,1)S(1)} %dynamic-slice_bitcast_fusion), channel_id=1, source_target_pairs={{0,0},{32,3},{64,8},{96,11},{128,16},{160,19},{192,24},{224,27},{3... | collective-permute-start | bytes 786440 | tf_op jit(solution)/shard_map/ppermute | solution.py:174
  12.0 17.8 %collective-permute-start.3 = (bf16[2,256,256]{2,1,0:T(8,128)(2,1)S(1)}, bf16[2,256,256]{2,1,0:T(8,128)(2,1)S(1)}, u32[]{:S(2)}, u32[]{:S(2)}) collective-permute-start(bf16[2,256,256]{2,1,0:T(8,128)(2,1)S(1)} %collective-permute-done), channel_id=1, source_target_pairs={{0,6},{3,5},{8,14},{11,13},{16,22},{19,21},{24,30},{27,29},{36,34}... | collective-permute-start | bytes 786440 | tf_op jit(solution)/shard_map/ppermute | solution.py:181
  12.7 17.2 %collective-permute-start.2 = (bf16[2,256,256]{2,1,0:T(8,128)(2,1)S(1)}, bf16[2,256,256]{2,1,0:T(8,128)(2,1)S(1)}, u32[]{:S(2)}, u32[]{:S(2)}) collective-permute-start(bf16[2,256,256]{2,1,0:T(8,128)(2,1)S(1)} %collective-permute-done), channel_id=1, source_target_pairs={{0,7},{3,2},{8,15},{11,10},{16,23},{19,18},{24,31},{27,26},{36,35}... | collective-permute-start | bytes 786440 | tf_op jit(solution)/shard_map/ppermute | solution.py:181
  13.4 16.5 %collective-permute-start.1 = (bf16[2,256,256]{2,1,0:T(8,128)(2,1)S(1)}, bf16[2,256,256]{2,1,0:T(8,128)(2,1)S(1)}, u32[]{:S(2)}, u32[]{:S(2)}) collective-permute-start(bf16[2,256,256]{2,1,0:T(8,128)(2,1)S(1)} %collective-permute-done), channel_id=1, source_target_pairs={{0,1},{3,4},{8,9},{11,12},{16,17},{19,20},{24,25},{27,28},{36,37},... | collective-permute-start | bytes 786440 | tf_op jit(solution)/shard_map/ppermute | solution.py:181
  14.7 26.6 %all-to-all-start = ((bf16[32,2,8,256]{3,2,1,0:T(8,128)(2,1)}), bf16[32,2,8,256]{3,2,1,0:T(8,128)(2,1)S(1)}, u32[]{:S(2)}, u32[]{:S(2)}) async-start(bf16[32,2,8,256]{3,2,1,0:T(8,128)(2,1)} %bitcast.11), calls=%async_computation | async-start | bytes 524288 | tf_op jit(solution)/shard_map/all_to_all | solution.py:200
  30.0 16.2 %collective-permute-start.6 = (bf16[2,256,256]{2,1,0:T(8,128)(2,1)S(1)}, bf16[2,256,256]{2,1,0:T(8,128)(2,1)S(1)}, u32[]{:S(2)}, u32[]{:S(2)}) collective-permute-start(bf16[2,256,256]{2,1,0:T(8,128)(2,1)S(1)} %add_add_fusion.r0), channel_id=1, source_target_pairs={{0,24},{8,0},{16,8},{24,16},{1,25},{9,1},{17,9},{25,17},{2,26},{10... | collective-permute-start | bytes 786440 | tf_op jit(solution)/shard_map/ppermute | solution.py:185
  32.5 13.7 %collective-permute-start.5 = (bf16[2,256,256]{2,1,0:T(8,128)(2,1)S(1)}, bf16[2,256,256]{2,1,0:T(8,128)(2,1)S(1)}, u32[]{:S(2)}, u32[]{:S(2)}) collective-permute-start(bf16[2,256,256]{2,1,0:T(8,128)(2,1)S(1)} %add_add_fusion.r0), channel_id=1, source_target_pairs={{0,16},{8,24},{16,0},{24,8},{1,17},{9,25},{17,1},{25,9},{2,18},{10... | collective-permute-start | bytes 786440 | tf_op jit(solution)/shard_map/ppermute | solution.py:185
  33.1 16.7 %collective-permute-start.4 = (bf16[2,256,256]{2,1,0:T(8,128)(2,1)S(1)}, bf16[2,256,256]{2,1,0:T(8,128)(2,1)S(1)}, u32[]{:S(2)}, u32[]{:S(2)}) collective-permute-start(bf16[2,256,256]{2,1,0:T(8,128)(2,1)S(1)} %add_add_fusion.r0), channel_id=1, source_target_pairs={{0,8},{8,16},{16,24},{24,0},{1,9},{9,17},{17,25},{25,1},{2,10},{10... | collective-permute-start | bytes 786440 | tf_op jit(solution)/shard_map/ppermute | solution.py:185
  37.9 1.3 %copy-start.2 = (bf16[2,256,2048]{2,1,0:T(8,128)(2,1)}, bf16[2,256,2048]{2,1,0:T(8,128)(2,1)S(1)}, u32[]{:S(2)}) copy-start(bf16[2,256,2048]{2,1,0:T(8,128)(2,1)S(1)} %mix_send.1.mixed) | copy-start | bytes 6291460
  49.7 1.6 %copy-start.3 = (bf16[2,256,2048]{2,1,0:T(8,128)(2,1)S(1)}, bf16[2,256,2048]{2,1,0:T(8,128)(2,1)}, u32[]{:S(2)}) copy-start(bf16[2,256,2048]{2,1,0:T(8,128)(2,1)} %copy-done.2) | copy-start | bytes 6291460
  53.2 9.7 %collective-permute-start.7 = (bf16[32,16,512]{2,1,0:T(8,128)(2,1)S(1)}, bf16[32,16,512]{2,1,0:T(8,128)(2,1)S(1)}, u32[]{:S(2)}, u32[]{:S(2)}) collective-permute-start(bf16[32,16,512]{2,1,0:T(8,128)(2,1)S(1)} %get-tuple-element.8), channel_id=1, source_target_pairs={{0,32},{32,0},{1,33},{33,1},{2,34},{34,2},{3,35},{35,3},{4,36},{36... | collective-permute-start | bytes 1572872 | tf_op jit(solution)/shard_map/ppermute | solution.py:205
  59.4 2.2 %copy-start = (bf16[4,256,2048]{2,1,0:T(8,128)(2,1)S(1)}, bf16[4,256,2048]{2,1,0:T(8,128)(2,1)}, u32[]{:S(2)}) copy-start(bf16[4,256,2048]{2,1,0:T(8,128)(2,1)} %mix_keep.1.mixed) | copy-start | bytes 12582916
  84.0 2.8 %collective-permute-start.10 = (f32[16,512]{1,0:T(8,128)S(1)}, f32[16,512]{1,0:T(8,128)S(1)}, u32[]{:S(2)}, u32[]{:S(2)}) collective-permute-start(f32[16,512]{1,0:T(8,128)S(1)} %convert_reduce_fusion), channel_id=1, source_target_pairs={{0,192},{64,0},{128,64},{192,128},{1,193},{65,1},{129,65},{193,129... | collective-permute-start | bytes 98312 | tf_op jit(solution)/shard_map/ppermute | solution.py:212
  84.1 4.4 %collective-permute-start.9 = (f32[16,512]{1,0:T(8,128)S(1)}, f32[16,512]{1,0:T(8,128)S(1)}, u32[]{:S(2)}, u32[]{:S(2)}) collective-permute-start(f32[16,512]{1,0:T(8,128)S(1)} %convert_reduce_fusion), channel_id=1, source_target_pairs={{0,128},{64,192},{128,0},{192,64},{1,129},{65,193},{129,1},{193,65... | collective-permute-start | bytes 98312 | tf_op jit(solution)/shard_map/ppermute | solution.py:212
  85.4 4.0 %collective-permute-start.8 = (f32[16,512]{1,0:T(8,128)S(1)}, f32[16,512]{1,0:T(8,128)S(1)}, u32[]{:S(2)}, u32[]{:S(2)}) collective-permute-start(f32[16,512]{1,0:T(8,128)S(1)} %convert_reduce_fusion), channel_id=1, source_target_pairs={{0,64},{64,128},{128,192},{192,0},{1,65},{65,129},{129,193},{193,1... | collective-permute-start | bytes 98312 | tf_op jit(solution)/shard_map/ppermute | solution.py:212
  89.4 5.4 %collective-permute-start.11 = (bf16[16,512]{1,0:T(8,128)(2,1)S(1)}, bf16[16,512]{1,0:T(8,128)(2,1)S(1)}, u32[]{:S(2)}, u32[]{:S(2)}) collective-permute-start(bf16[16,512]{1,0:T(8,128)(2,1)S(1)} %add_convert_fusion.1), channel_id=1, source_target_pairs={{0,32},{32,0},{1,33},{33,1},{2,34},{34,2},{3,35},{35,3},{4,36},{36... | collective-permute-start | bytes 49160 | tf_op jit(solution)/shard_map/ppermute | solution.py:214
where the time goes:
time: 95.9 us; the launch traced here: 95.5 us
  starting transfers between devices  35.8 us (37%)
  blocking collectives  20.8 us (22%)
  waiting for transfers between devices  18.4 us (19%)
  Pallas kernels  13 us (14%)
  local copies, waits for them, and re-layouts  6.85 us (7%)
    all_to_all x1, blocking collectives, contract(): lax.all_to_all(pair, ('x', 'z'), split_axis=0, concat_axis=0, tiled=True)  20.8 us
    all_to_all x1, starting transfers between devices, contract(): lax.all_to_all(by_time, ('x', 'z'), split_axis=0, concat_axis=0, tiled=True)  15.2 us
    pallas_call x2, Pallas kernels, mix(): pl.pallas_call(functools.partial(mix_kernel, keep), grid=(N // CHUNK,), o...  9.89 us
    ppermute x3, waiting for transfers between devices, spread(): pieces[d] = lax.ppermute(part, 'x', [(i, (i + d) % NX) for i in range(NX)])  8.43 us
    ppermute x1, starting transfers between devices, spread(): got = [lax.ppermute(own, ALL, turns)]  7.64 us
    unnamed x18, local copies, waits for them, and re-layouts  5.13 us
    ppermute x1, starting transfers between devices, contract(): other = lax.ppermute(mine, 'core', [(0, 1), (1, 0)])  4.57 us
    ppermute x3, waiting for transfers between devices, contract(): lax.ppermute(one, 'y', [(i, (i + d) % NY) for i in range(NY)])  3.82 us
  transfers between devices with their start and end apart: 13, of which 8 were waited for; matrix products, arithmetic and copies ran while one was open for 0% of the time, Pallas kernels for 12%

commit v1 on v0

--- a/solution.py
+++ b/solution.py
@@ -195,7 +195,6 @@
 
 
 def contract(peram, meson_blocks, edges):
-    core = lax.axis_index("core")
     by_time = jnp.swapaxes(peram[0], 2, 3)
     tau_t = lax.all_to_all(by_time, ("x", "z"), split_axis=0, concat_axis=0, tiled=True)
     mixed_keep = mix(True, *edges, meson_blocks)
@@ -207,14 +206,11 @@
     pair = (keep + got.astype(F32)).astype(BF16)
     times = lax.all_to_all(pair, ("x", "z"), split_axis=0, concat_axis=0, tiled=True)
     one = jnp.sum(times.astype(F32), 0)
-    total = one
-    for d in range(1, NY):
-        total = total + lax.ppermute(one, "y", [(i, (i + d) % NY) for i in range(NY)])
-    mine = total.astype(BF16)
-    other = lax.ppermute(mine, "core", [(0, 1), (1, 0)])
-    halves = jnp.where(core == 0, jnp.stack([mine, other]), jnp.stack([other, mine]))
-    halves = halves.reshape(2, 2, ROWS, 2, N)
-    return jnp.transpose(halves, (2, 0, 1, 3, 4)).reshape(ROWS, NODES, 2, N)
+    one = one.astype(BF16)
+    copies = jnp.broadcast_to(one[None], (NY * NC,) + one.shape)
+    every = lax.all_to_all(copies, ("y", "core"), split_axis=0, concat_axis=0, tiled=True)
+    total = jnp.sum(every.astype(F32).reshape(NY, NC, 2, ROWS, 2, N), 0)
+    return jnp.transpose(total, (2, 0, 1, 3, 4)).reshape(ROWS, NODES, 2, N).astype(BF16)
 
 
 def solution(mesh):

time: 95.9 us -> 95.6 us (level)
  the two profiles are of different devices: /device:TPU:1 before, /device:TPU:32 now
where the time goes in v1:
time: 95.6 us; the launch traced here: 95.2 us
  blocking collectives  33.5 us (35%)
  starting transfers between devices  31.4 us (33%)
  Pallas kernels  13 us (14%)
  waiting for transfers between devices  9.91 us (10%)
  local copies, waits for them, and re-layouts  6.84 us (7%)
    all_to_all x1, blocking collectives, contract(): lax.all_to_all(pair, ('x', 'z'), split_axis=0, concat_axis=0, tiled=True)  25 us
    all_to_all x1, starting transfers between devices, contract(): lax.all_to_all(by_time, ('x', 'z'), split_axis=0, concat_axis=0, tiled=True)  23.5 us
    pallas_call x2, Pallas kernels, mix(): pl.pallas_call(functools.partial(mix_kernel, keep), grid=(N // CHUNK,), o...  9.92 us
    all_to_all x1, blocking collectives, contract(): lax.all_to_all(copies, ('y', 'core'), split_axis=0, concat_axis=0, tiled=...  8.49 us
    ppermute x3, waiting for transfers between devices, spread(): pieces[d] = lax.ppermute(part, 'x', [(i, (i + d) % NX) for i in range(NX)])  6.59 us
    unnamed x18, local copies, waits for them, and re-layouts  5.14 us
    ppermute x3, starting transfers between devices, spread(): pieces[d] = lax.ppermute(part, 'x', [(i, (i + d) % NX) for i in range(NX)])  4.47 us
    all_to_all x1, waiting for transfers between devices, contract(): lax.all_to_all(by_time, ('x', 'z'), split_axis=0, concat_axis=0, tiled=True)  3.31 us
  transfers between devices with their start and end apart: 9, of which 3 were waited for; matrix products, arithmetic and copies ran while one was open for 0% of the time, Pallas kernels for 12%

profile of v1, /device:TPU:32, one launch (start us, length us, event | category | flops | bytes accessed | tf_op | source)
XLA Modules:
  0.0 95.2 jit_solution(13599980001761015338)
XLA Ops:
  0.0 0.0 copy-start.1
  0.0 0.0 copy-start.8
  0.0 0.0 copy-start.7
  0.0 0.0 copy-start.6
  0.0 0.0 copy-start.5
  0.0 0.0 copy-start.4
  0.1 1.1 %dynamic-slice_bitcast_fusion = bf16[2,256,256]{2,1,0:T(8,128)(2,1)S(1)} fusion(bf16[1,4,2,256,256]{4,3,2,1,0:T(8,128)(2,1)} %blocks.3, s32[]{:T(128)S(6)} %select_n.4), kind=kLoop, calls=%fused_computation.2 | loop fusion | bytes 524292 | tf_op jit(solution)/shard_map/jit(dynamic_index_in_dim)/squeeze | solution.py:168
  1.1 0.7 collective-permute-start
  1.8 0.0 collective-permute-done
  1.8 0.7 collective-permute-start.3
  2.5 0.7 collective-permute-start.2
  3.2 1.3 %collective-permute-start.1 = (bf16[2,256,256]{2,1,0:T(8,128)(2,1)S(1)}, bf16[2,256,256]{2,1,0:T(8,128)(2,1)S(1)}, u32[]{:S(2)}, u32[]{:S(2)}) collective-permute-start(bf16[2,256,256]{2,1,0:T(8,128)(2,1)S(1)} %collective-permute-done), channel_id=1, source_target_pairs={{0,1},{3,4},{8,9},{11,12},{16,17},{19,20},{24,25},{27,28},{36,37},... | collective-permute-start | bytes 786440 | tf_op jit(solution)/shard_map/ppermute | solution.py:181
  4.5 23.5 %all-to-all-start = ((bf16[32,2,8,256]{3,2,1,0:T(8,128)(2,1)}), bf16[32,2,8,256]{3,2,1,0:T(8,128)(2,1)S(1)}, u32[]{:S(2)}, u32[]{:S(2)}) async-start(bf16[32,2,8,256]{3,2,1,0:T(8,128)(2,1)} %bitcast.13), calls=%async_computation | async-start | bytes 524288 | tf_op jit(solution)/shard_map/all_to_all | solution.py:199
  28.0 0.0 collective-permute-done.3
  28.0 0.0 collective-permute-done.2
  28.0 0.0 collective-permute-done.1
  28.0 0.1 add_add_fusion.r0
  28.1 2.8 %collective-permute-start.6 = (bf16[2,256,256]{2,1,0:T(8,128)(2,1)S(1)}, bf16[2,256,256]{2,1,0:T(8,128)(2,1)S(1)}, u32[]{:S(2)}, u32[]{:S(2)}) collective-permute-start(bf16[2,256,256]{2,1,0:T(8,128)(2,1)S(1)} %add_add_fusion.r0), channel_id=1, source_target_pairs={{0,24},{8,0},{16,8},{24,16},{1,25},{9,1},{17,9},{25,17},{2,26},{10... | collective-permute-start | bytes 786440 | tf_op jit(solution)/shard_map/ppermute | solution.py:185
  30.9 0.8 collective-permute-start.5
  31.7 0.9 collective-permute-start.4
  32.5 0.0 copy-done.1
  32.6 0.0 copy-done.8
  32.6 0.0 copy-done.7
  32.6 0.0 copy-done.6
  32.6 0.0 copy-done.5
  32.6 0.0 copy-done.4
  32.6 4.2 %mix_send.1.mixed = bf16[2,256,2048]{2,1,0:T(8,128)(2,1)S(1)} custom-call(s32[1,1,32]{2,1,0:T(1,128)S(1)} %copy-done.5, s32[1,1,32]{2,1,0:T(1,128)S(1)} %copy-done.6, s32[1,1,32]{2,1,0:T(1,128)S(1)} %copy-done.7, s32[1,1,32]{2,1,0:T(1,128)S(1)} %copy-done.8, f32[2,16]{1,0:T(2,128)S(1)} %bitcast.11, bf16[1,4,2,256,256]{4,3,2,1,0:T(8,128)(2,1)S(1)} %copy-done.1), custom_call_target="tpu_custom_call" | custom-call | flops 16777216 | bytes 3145728 | tf_op jit(solution)/shard_map/mix_send/pallas_call | solution.py:80
  36.8 0.0 copy-start.2
  36.8 1.3 %copy-done.2 = bf16[2,256,2048]{2,1,0:T(8,128)(2,1)} copy-done((bf16[2,256,2048]{2,1,0:T(8,128)(2,1)}, bf16[2,256,2048]{2,1,0:T(8,128)(2,1)S(1)}, u32[]{:S(2)}) %copy-start.2) | copy-done | bytes 2097176
  38.1 3.3 %all-to-all-done.tau_t = bf16[32,2,8,256]{3,2,1,0:T(8,128)(2,1)S(1)} async-done(((bf16[32,2,8,256]{3,2,1,0:T(8,128)(2,1)}), bf16[32,2,8,256]{3,2,1,0:T(8,128)(2,1)S(1)}, u32[]{:S(2)}, u32[]{:S(2)}) %all-to-all-start) | async-done | bytes 262176 | tf_op jit(solution)/shard_map/all_to_all | solution.py:199
  41.5 3.3 %collective-permute-done.6.r3 = bf16[2,256,256]{2,1,0:T(8,128)(2,1)S(1)} collective-permute-done((bf16[2,256,256]{2,1,0:T(8,128)(2,1)S(1)}, bf16[2,256,256]{2,1,0:T(8,128)(2,1)S(1)}, u32[]{:S(2)}, u32[]{:S(2)}) %collective-permute-start.6) | collective-permute-done | bytes 262176 | tf_op jit(solution)/shard_map/ppermute | solution.py:185
  44.8 0.0 collective-permute-done.5.r2
  44.8 3.3 %collective-permute-done.4.r1 = bf16[2,256,256]{2,1,0:T(8,128)(2,1)S(1)} collective-permute-done((bf16[2,256,256]{2,1,0:T(8,128)(2,1)S(1)}, bf16[2,256,256]{2,1,0:T(8,128)(2,1)S(1)}, u32[]{:S(2)}, u32[]{:S(2)}) %collective-permute-start.4) | collective-permute-done | bytes 262176 | tf_op jit(solution)/shard_map/ppermute | solution.py:185
  48.0 0.0 copy-start.3
  48.0 1.6 %copy-done.3 = bf16[2,256,2048]{2,1,0:T(8,128)(2,1)S(1)} copy-done((bf16[2,256,2048]{2,1,0:T(8,128)(2,1)S(1)}, bf16[2,256,2048]{2,1,0:T(8,128)(2,1)}, u32[]{:S(2)}) %copy-start.3) | copy-done | bytes 2097176
  49.6 1.8 %send_half.1 = (bf16[32,16,512]{2,1,0:T(8,128)(2,1)S(1)}, bf16[2048,512]{1,0:T(8,128)(2,1)S(1)}) custom-call(bf16[32,2,8,256]{3,2,1,0:T(8,128)(2,1)S(1)} %all-to-all-done.tau_t, bf16[2,256,256]{2,1,0:T(8,128)(2,1)S(1)} %add_add_fusion.r0, bf16[2,256,256]{2,1,0:T(8,128)(2,1)S(1)} %collective-permute-done.4.r1, ...), custom_call_target="tpu_custom_call" | custom-call | flops 1610612736 | bytes 6291456 | tf_op jit(solution)/shard_map/send_half/pallas_call | solution.py:126
  51.5 0.1 collective-permute-start.7
  51.6 5.7 %mix_keep.1.mixed = bf16[4,256,2048]{2,1,0:T(8,128)(2,1)} custom-call(s32[1,1,32]{2,1,0:T(1,128)} %left_e.3, s32[1,1,32]{2,1,0:T(1,128)} %right_e.3, s32[1,1,32]{2,1,0:T(1,128)} %node_e.3, s32[1,1,32]{2,1,0:T(1,128)} %weight_e.3, f32[2,16]{1,0:T(2,128)} %bitcast.10, bf16[1,4,2,256,256]{4,3,2,1,0:T(8,128)(2,1)} %blocks.3), custom_call_target="tpu_custom_call" | custom-call | flops 16777216 | bytes 3145728 | tf_op jit(solution)/shard_map/mix_keep/pallas_call | solution.py:80
  57.3 0.0 copy-start
  57.3 2.2 %copy-done = bf16[4,256,2048]{2,1,0:T(8,128)(2,1)S(1)} copy-done((bf16[4,256,2048]{2,1,0:T(8,128)(2,1)S(1)}, bf16[4,256,2048]{2,1,0:T(8,128)(2,1)}, u32[]{:S(2)}) %copy-start) | copy-done | bytes 4194328
  59.5 1.2 %keep_half.1 = f32[32,16,512]{2,1,0:T(8,128)S(1)} custom-call(bf16[4,256,2048]{2,1,0:T(8,128)(2,1)S(1)} %copy-done, bf16[2048,512]{1,0:T(8,128)(2,1)S(1)} %get-tuple-element.7.stack), custom_call_target="tpu_custom_call" | custom-call | flops 1073741824 | bytes 5242880 | tf_op jit(solution)/shard_map/keep_half/pallas_call | solution.py:146
  60.7 0.0 collective-permute-done.7
  60.7 0.2 add_convert_fusion
  60.9 25.0 %all_to_all.15 = bf16[32,16,512]{2,1,0:T(8,128)(2,1)S(1)} all-to-all(bf16[32,16,512]{2,1,0:T(8,128)(2,1)S(1)} %add_convert_fusion), channel_id=1, replica_groups=mesh['y'=4,'core'=2,'x'=4,'z'=8] {'x','z'}, dimensions={0} | all-to-all | bytes 1048576 | tf_op jit(solution)/shard_map/all_to_all | solution.py:207
  85.9 0.1 reduce_sum.21
  86.0 8.5 %all_to_all.16 = bf16[8,16,512]{2,1,0:T(8,128)(2,1)S(1)} all-to-all(bf16[8,16,512]{2,1,0:T(8,128)(2,1)S(1)} %broadcast_in_dim.2), channel_id=1, replica_groups=mesh['y'=4,'core'=2,'x'=4,'z'=8] {'y','core'}, dimensions={0} | all-to-all | bytes 262144 | tf_op jit(solution)/shard_map/all_to_all | solution.py:211
  94.6 0.6 copy.8
  (2 shorter events, 0.0 us)
Async XLA Ops:
  0.0 32.6 %copy-start.1 = (bf16[1,4,2,256,256]{4,3,2,1,0:T(8,128)(2,1)S(1)}, bf16[1,4,2,256,256]{4,3,2,1,0:T(8,128)(2,1)}, u32[]{:S(2)}) copy-start(bf16[1,4,2,256,256]{4,3,2,1,0:T(8,128)(2,1)} %blocks.3) | copy-start | bytes 3145732
  0.0 32.6 %copy-start.8 = (s32[1,1,32]{2,1,0:T(1,128)S(1)}, s32[1,1,32]{2,1,0:T(1,128)}, u32[]{:S(2)}) copy-start(s32[1,1,32]{2,1,0:T(1,128)} %weight_e.3) | copy-start | bytes 388
  0.0 32.6 %copy-start.7 = (s32[1,1,32]{2,1,0:T(1,128)S(1)}, s32[1,1,32]{2,1,0:T(1,128)}, u32[]{:S(2)}) copy-start(s32[1,1,32]{2,1,0:T(1,128)} %node_e.3) | copy-start | bytes 388
  0.0 32.5 %copy-start.6 = (s32[1,1,32]{2,1,0:T(1,128)S(1)}, s32[1,1,32]{2,1,0:T(1,128)}, u32[]{:S(2)}) copy-start(s32[1,1,32]{2,1,0:T(1,128)} %right_e.3) | copy-start | bytes 388
  0.0 32.5 %copy-start.5 = (s32[1,1,32]{2,1,0:T(1,128)S(1)}, s32[1,1,32]{2,1,0:T(1,128)}, u32[]{:S(2)}) copy-start(s32[1,1,32]{2,1,0:T(1,128)} %left_e.3) | copy-start | bytes 388
  0.0 32.5 %copy-start.4 = (f32[16,2]{0,1:T(2,128)S(1)}, f32[16,2]{0,1:T(2,128)}, u32[]{:S(2)}) copy-start(f32[16,2]{0,1:T(2,128)} %param.13) | copy-start | bytes 388
  1.1 0.7 collective-permute-start
  1.8 26.2 %collective-permute-start.3 = (bf16[2,256,256]{2,1,0:T(8,128)(2,1)S(1)}, bf16[2,256,256]{2,1,0:T(8,128)(2,1)S(1)}, u32[]{:S(2)}, u32[]{:S(2)}) collective-permute-start(bf16[2,256,256]{2,1,0:T(8,128)(2,1)S(1)} %collective-permute-done), channel_id=1, source_target_pairs={{0,6},{3,5},{8,14},{11,13},{16,22},{19,21},{24,30},{27,29},{36,34}... | collective-permute-start | bytes 786440 | tf_op jit(solution)/shard_map/ppermute | solution.py:181
  2.5 25.5 %collective-permute-start.2 = (bf16[2,256,256]{2,1,0:T(8,128)(2,1)S(1)}, bf16[2,256,256]{2,1,0:T(8,128)(2,1)S(1)}, u32[]{:S(2)}, u32[]{:S(2)}) collective-permute-start(bf16[2,256,256]{2,1,0:T(8,128)(2,1)S(1)} %collective-permute-done), channel_id=1, source_target_pairs={{0,7},{3,2},{8,15},{11,10},{16,23},{19,18},{24,31},{27,26},{36,35}... | collective-permute-start | bytes 786440 | tf_op jit(solution)/shard_map/ppermute | solution.py:181
  3.2 24.8 %collective-permute-start.1 = (bf16[2,256,256]{2,1,0:T(8,128)(2,1)S(1)}, bf16[2,256,256]{2,1,0:T(8,128)(2,1)S(1)}, u32[]{:S(2)}, u32[]{:S(2)}) collective-permute-start(bf16[2,256,256]{2,1,0:T(8,128)(2,1)S(1)} %collective-permute-done), channel_id=1, source_target_pairs={{0,1},{3,4},{8,9},{11,12},{16,17},{19,20},{24,25},{27,28},{36,37},... | collective-permute-start | bytes 786440 | tf_op jit(solution)/shard_map/ppermute | solution.py:181
  4.5 37.0 %all-to-all-start = ((bf16[32,2,8,256]{3,2,1,0:T(8,128)(2,1)}), bf16[32,2,8,256]{3,2,1,0:T(8,128)(2,1)S(1)}, u32[]{:S(2)}, u32[]{:S(2)}) async-start(bf16[32,2,8,256]{3,2,1,0:T(8,128)(2,1)} %bitcast.13), calls=%async_computation | async-start | bytes 524288 | tf_op jit(solution)/shard_map/all_to_all | solution.py:199
  28.1 16.7 %collective-permute-start.6 = (bf16[2,256,256]{2,1,0:T(8,128)(2,1)S(1)}, bf16[2,256,256]{2,1,0:T(8,128)(2,1)S(1)}, u32[]{:S(2)}, u32[]{:S(2)}) collective-permute-start(bf16[2,256,256]{2,1,0:T(8,128)(2,1)S(1)} %add_add_fusion.r0), channel_id=1, source_target_pairs={{0,24},{8,0},{16,8},{24,16},{1,25},{9,1},{17,9},{25,17},{2,26},{10... | collective-permute-start | bytes 786440 | tf_op jit(solution)/shard_map/ppermute | solution.py:185
  30.9 13.9 %collective-permute-start.5 = (bf16[2,256,256]{2,1,0:T(8,128)(2,1)S(1)}, bf16[2,256,256]{2,1,0:T(8,128)(2,1)S(1)}, u32[]{:S(2)}, u32[]{:S(2)}) collective-permute-start(bf16[2,256,256]{2,1,0:T(8,128)(2,1)S(1)} %add_add_fusion.r0), channel_id=1, source_target_pairs={{0,16},{8,24},{16,0},{24,8},{1,17},{9,25},{17,1},{25,9},{2,18},{10... | collective-permute-start | bytes 786440 | tf_op jit(solution)/shard_map/ppermute | solution.py:185
  31.7 16.4 %collective-permute-start.4 = (bf16[2,256,256]{2,1,0:T(8,128)(2,1)S(1)}, bf16[2,256,256]{2,1,0:T(8,128)(2,1)S(1)}, u32[]{:S(2)}, u32[]{:S(2)}) collective-permute-start(bf16[2,256,256]{2,1,0:T(8,128)(2,1)S(1)} %add_add_fusion.r0), channel_id=1, source_target_pairs={{0,8},{8,16},{16,24},{24,0},{1,9},{9,17},{17,25},{25,1},{2,10},{10... | collective-permute-start | bytes 786440 | tf_op jit(solution)/shard_map/ppermute | solution.py:185
  36.8 1.3 %copy-start.2 = (bf16[2,256,2048]{2,1,0:T(8,128)(2,1)}, bf16[2,256,2048]{2,1,0:T(8,128)(2,1)S(1)}, u32[]{:S(2)}) copy-start(bf16[2,256,2048]{2,1,0:T(8,128)(2,1)S(1)} %mix_send.1.mixed) | copy-start | bytes 6291460
  48.0 1.6 %copy-start.3 = (bf16[2,256,2048]{2,1,0:T(8,128)(2,1)S(1)}, bf16[2,256,2048]{2,1,0:T(8,128)(2,1)}, u32[]{:S(2)}) copy-start(bf16[2,256,2048]{2,1,0:T(8,128)(2,1)} %copy-done.2) | copy-start | bytes 6291460
  51.5 9.3 %collective-permute-start.7 = (bf16[32,16,512]{2,1,0:T(8,128)(2,1)S(1)}, bf16[32,16,512]{2,1,0:T(8,128)(2,1)S(1)}, u32[]{:S(2)}, u32[]{:S(2)}) collective-permute-start(bf16[32,16,512]{2,1,0:T(8,128)(2,1)S(1)} %get-tuple-element.8), channel_id=1, source_target_pairs={{0,32},{32,0},{1,33},{33,1},{2,34},{34,2},{3,35},{35,3},{4,36},{36... | collective-permute-start | bytes 1572872 | tf_op jit(solution)/shard_map/ppermute | solution.py:204
  57.3 2.2 %copy-start = (bf16[4,256,2048]{2,1,0:T(8,128)(2,1)S(1)}, bf16[4,256,2048]{2,1,0:T(8,128)(2,1)}, u32[]{:S(2)}) copy-start(bf16[4,256,2048]{2,1,0:T(8,128)(2,1)} %mix_keep.1.mixed) | copy-start | bytes 12582916
